TPU v7x, 32 devices: a whole 2x2x4 slice. The times are simulated.
32 devices in a mesh: expert: 8 (over z, x), width: 4 (over y, core).
Axes of the slice: x: 2, y: 2, z: 4, core: 2. Of those that a mesh axis runs over, the one named last changes fastest.
Arguments:
- tokens: bfloat16 [1024, 4096], P('expert'), may hold values from -6 to 6
- expert_ids: int32 [1024, 8], P('expert'), may hold values from 0 to 15, all different within a row; in each aligned block of 128 rows (0 to 127, 128 to 255, ...) at most 128 rows name the same one
- combine_weights: float32 [1024, 8], P('expert'), may hold values from 0.05 to 0.3
- gate_weight: bfloat16 [16, 4096, 1536], P('expert', None, 'width'), may hold values from -0.09375 to 0.09375
- up_weight: bfloat16 [16, 4096, 1536], P('expert', None, 'width'), may hold values from -0.09375 to 0.09375
- down_weight: bfloat16 [16, 1536, 4096], P('expert', 'width'), may hold values from -0.15625 to 0.15625
Outputs:
- mixed: bfloat16 [1024, 4096], P('expert', 'width')
Inputs may be any that keep to these rules, and one draw needn't show every extreme that they name: `expert_ids`: each token names 8 different experts. Within the tokens of one index of expert (aligned blocks of 128 tokens) no expert is named by more than 128 tokens, a bound that some block reaches.
All inputs are finite; a program needn't handle non-finite values.
Results may differ from a plain program's by a relative error of at most 0.012.
Values may be sent and summed in bfloat16 or wider, within the bound.
A program may use at most 128 MiB of HBM per device.

v0:
```python
import jax
import jax.numpy as jnp
from jax import lax
from jax.sharding import PartitionSpec as P


def local(tokens, expert_ids, combine_weights, gate_weight, up_weight, down_weight):
    tok_rows = tokens.shape[0]
    top_count = expert_ids.shape[1]
    exp_local = gate_weight.shape[0]
    n_expert = lax.axis_size("expert")
    n_width = lax.axis_size("width")
    experts_all = exp_local * n_expert
    slots = 2 * tok_rows * top_count // experts_all
    width_all = tokens.shape[1]
    cols = width_all // n_width
    flat_ids = expert_ids.reshape(-1)
    onehot = (flat_ids[:, None] == jnp.arange(experts_all, dtype=jnp.int32)[None, :]).astype(
        jnp.int32
    )
    rank = jnp.sum(jnp.cumsum(onehot, axis=0) * onehot, axis=1) - 1
    slot = flat_ids * slots + rank
    token_index = jnp.arange(tok_rows * top_count, dtype=jnp.int32) // top_count
    table = jnp.full((experts_all * slots,), tok_rows, jnp.int32).at[slot].set(token_index)
    padded = jnp.concatenate([tokens, jnp.zeros((1, width_all), jnp.bfloat16)], axis=0)
    outgoing = padded[table].reshape(n_expert, exp_local, slots, width_all)
    own_cols = lax.dynamic_slice_in_dim(outgoing, lax.axis_index("width") * cols, cols, 3)
    arrived_cols = lax.all_to_all(own_cols, "expert", split_axis=0, concat_axis=0, tiled=True)
    arrived = lax.all_gather(arrived_cols, "width", axis=3, tiled=True)
    gate = jnp.einsum("skmd,kdf->skmf", arrived, gate_weight, preferred_element_type=jnp.float32)
    up_part = jnp.einsum("skmd,kdf->skmf", arrived, up_weight, preferred_element_type=jnp.float32)
    hidden = (jax.nn.silu(gate) * up_part).astype(jnp.bfloat16)
    partial_value = jnp.einsum(
        "skmf,kfd->skmd", hidden, down_weight, preferred_element_type=jnp.float32
    )
    reduced = lax.psum_scatter(
        partial_value.astype(jnp.bfloat16), "width", scatter_dimension=3, tiled=True
    ).astype(jnp.float32)
    returned = lax.all_to_all(
        reduced.astype(jnp.bfloat16), "expert", split_axis=0, concat_axis=0, tiled=True
    ).astype(reduced.dtype)
    picked = returned.reshape(experts_all * slots, cols)[slot].reshape(tok_rows, top_count, cols)
    mixed = jnp.sum(combine_weights[:, :, None] * picked, axis=1)
    return mixed.astype(jnp.bfloat16)


def solution(mesh):
    placed = (
        P("expert", None),
        P("expert", None),
        P("expert", None),
        P("expert", None, "width"),
        P("expert", None, "width"),
        P("expert", "width", None),
    )
    return jax.shard_map(
        local, mesh=mesh, in_specs=placed, out_specs=P("expert", "width"), check_vma=False
    )
```

profile of v0, /device:TPU:0, one launch (start us, length us, event | category | flops | bytes accessed | tf_op | source)
XLA Modules:
  0.0 540.2 jit_solution(17724048829518535215)
XLA Ops:
  6.5 0.8 copy.20
  7.3 0.1 eq.29
  7.4 0.1 eq.25
  7.5 0.7 broadcast_multiply_fusion
  8.2 4.5 reduce-window.6
  12.7 0.1 slice.12
  12.8 0.1 copy.22
  13.0 0.1 copy.23
  13.1 0.1 broadcast_add_fusion
  13.2 0.1 copy.19
  13.3 0.1 mul.40
  13.4 4.3 scatter_custom_fusion
  17.7 1.3 concatenate.3
  19.1 14.3 %gather_fusion = bf16[2048,4096]{1,0:T(8,128)(2,1)} fusion(bf16[129,4096]{1,0:T(8,128)(2,1)S(1)} %concatenate.3, s32[2048]{0:T(1024)S(1)} %fusion.15), kind=kCustom, calls=%fused_computation | custom fusion | bytes 33562624 | tf_op jit(solution)/shard_map/gather | solution.py:26
  33.4 2.6 constant_dynamic-slice_fusion
  36.0 100.3 %all_to_all.10 = bf16[8,2,128,1024]{3,2,1,0:T(8,128)(2,1)S(1)} all-to-all(bf16[8,2,128,1024]{3,2,1,0:T(8,128)(2,1)S(1)} %constant_dynamic-slice_fusion), channel_id=1, replica_groups=mesh['expert'=8,'width'=4] {'expert'}, dimensions={0} | all-to-all | bytes 8388608 | tf_op jit(solution)/shard_map/all_to_all | solution.py:28
  136.3 2.4 copy.24
  138.6 0.0 all-gather.2.cloned.1.call-update
  138.7 0.2 reduce-scatter.2.cloned.1.call-start
  138.9 104.9 %all-gather.2.cloned.1.call-done = bf16[8,2,128,4096]{3,2,0,1:T(8,128)(2,1)} async-done(((bf16[8,2,128,1024]{3,2,0,1:T(8,128)(2,1)}), bf16[8,2,128,4096]{3,2,0,1:T(8,128)(2,1)}) %all-gather.2.cloned.1.call-update) | async-done | bytes 16777232 | tf_op jit(solution)/shard_map/all_gather | solution.py:29
  243.8 14.1 %fusion.1 = f32[2,8,128,384]{3,2,1,0:T(8,128)S(1)} fusion(bf16[8,2,128,4096]{3,2,0,1:T(8,128)(2,1)} %all-gather.2.cloned.1.call-done, bf16[2,4096,384]{2,1,0:T(8,128)(2,1)} %param.10), kind=kOutput, calls=%fused_computation.5 | convolution fusion | flops 6442450944 | bytes 26214400 | tf_op jit(solution)/shard_map/skmd,kdf->skmf/dot_general | solution.py:31
  257.9 11.2 %fusion.6 = bf16[8,2,128,384]{3,2,0,1:T(8,128)(2,1)S(1)} fusion(f32[2,8,128,384]{3,2,1,0:T(8,128)S(1)} %fusion.1, bf16[8,2,128,4096]{3,2,0,1:T(8,128)(2,1)S(1)} %copy-done.1, bf16[2,4096,384]{2,1,0:T(8,128)(2,1)} %param.9), kind=kOutput, calls=%fused_computation.13 | convolution fusion | flops 6447169536 | bytes 27787264 | tf_op jit(solution)/shard_map/skmd,kdf->skmf/dot_general | solution.py:30
  269.2 15.2 %convert_bitcast_fusion = bf16[8,2,128,4096]{3,2,0,1:T(8,128)(2,1)} fusion(bf16[8,2,128,384]{3,2,0,1:T(8,128)(2,1)S(1)} %fusion.6, bf16[2,384,4096]{2,1,0:T(8,128)(2,1)} %param.11), kind=kOutput, calls=%fused_computation.3 | convolution fusion | flops 6450839552 | bytes 24641536 | tf_op jit(solution)/shard_map/skmf,kfd->skmd/dot_general | solution.py:33
  284.3 0.0 reduce-scatter.2.cloned.1.call-update
  284.3 125.0 %reduce-scatter.2.cloned.1.call-done = bf16[8,2,128,1024]{3,2,0,1:T(8,128)(2,1)} async-done(((bf16[8,2,128,4096]{3,2,0,1:T(8,128)(2,1)}), bf16[8,2,128,1024]{3,2,0,1:T(8,128)(2,1)}) %reduce-scatter.2.cloned.1.call-update) | async-done | bytes 4194320 | tf_op jit(solution)/shard_map/reduce_scatter | solution.py:36
  409.4 4.7 copy.25
  414.1 5.6 %all-to-all-start.1 = ((bf16[8,2,128,1024]{3,2,1,0:T(8,128)(2,1)}), bf16[8,2,128,1024]{3,2,1,0:T(8,128)(2,1)}, u32[]{:S(2)}, u32[]{:S(2)}) async-start(bf16[8,2,128,1024]{3,2,1,0:T(8,128)(2,1)} %copy.25), calls=%async_computation.2 | async-start | bytes 8388608 | tf_op jit(solution)/shard_map/all_to_all | solution.py:39
  419.8 0.1 copy.18
  419.9 93.0 %all-to-all-done.1 = bf16[8,2,128,1024]{3,2,1,0:T(8,128)(2,1)} async-done(((bf16[8,2,128,1024]{3,2,1,0:T(8,128)(2,1)}), bf16[8,2,128,1024]{3,2,1,0:T(8,128)(2,1)}, u32[]{:S(2)}, u32[]{:S(2)}) %all-to-all-start.1) | async-done | bytes 4194336 | tf_op jit(solution)/shard_map/all_to_all | solution.py:39
  512.9 6.5 %bitcast_convert_fusion = f32[2048,1024]{1,0:T(8,128)} fusion(bf16[8,2,128,1024]{3,2,1,0:T(8,128)(2,1)} %all-to-all-done.1), kind=kLoop, calls=%fused_computation.9 | loop fusion | flops 2097152 | bytes 12582912 | tf_op jit(solution)/shard_map/reshape | solution.py:42
  519.3 9.8 %gather_fusion.1 = f32[1024,1024]{1,0:T(8,128)} fusion(f32[2048,1024]{1,0:T(8,128)} %bitcast_convert_fusion, s32[1024]{0:T(1024)S(1)} %broadcast_clamp_fusion), kind=kCustom, calls=%fused_computation.1 | custom fusion | bytes 8392704 | tf_op jit(solution)/shard_map/gather | solution.py:42
  529.2 4.2 fusion.5
  (14 shorter events, 0.1 us)
Async XLA Ops:
  6.5 237.2 %all-gather.2.cloned.1.call-start = ((), (), s32[]{:S(2)}) async-start(), calls=%async_computation.3 | async-start | bytes 20971520 | tf_op jit(solution)/shard_map/all_gather | solution.py:29
  138.7 270.7 %reduce-scatter.2.cloned.1.call-start = ((), (), s32[]{:S(2)}) async-start(), calls=%async_computation.4 | async-start | bytes 20971520 | tf_op jit(solution)/shard_map/reduce_scatter | solution.py:36
  243.8 14.1 %copy-start.1 = (bf16[8,2,128,4096]{3,2,0,1:T(8,128)(2,1)S(1)}, bf16[8,2,128,4096]{3,2,0,1:T(8,128)(2,1)}, u32[]{:S(2)}) copy-start(bf16[8,2,128,4096]{3,2,0,1:T(8,128)(2,1)} %all-gather.2.cloned.1.call-done) | copy-start | bytes 50331652
  414.1 5.6 %copy-start = (f32[128,8]{0,1:T(8,128)S(1)}, f32[128,8]{0,1:T(8,128)}, u32[]{:S(2)}) copy-start(f32[128,8]{0,1:T(8,128)} %param.8) | copy-start | bytes 12292
  414.1 98.8 %all-to-all-start.1 = ((bf16[8,2,128,1024]{3,2,1,0:T(8,128)(2,1)}), bf16[8,2,128,1024]{3,2,1,0:T(8,128)(2,1)}, u32[]{:S(2)}, u32[]{:S(2)}) async-start(bf16[8,2,128,1024]{3,2,1,0:T(8,128)(2,1)} %copy.25), calls=%async_computation.2 | async-start | bytes 8388608 | tf_op jit(solution)/shard_map/all_to_all | solution.py:39
Sparse Core Ops, SparseCore 0:
  138.8 104.9 all-gather.1
  284.5 124.8 reduce-scatter.1
where the time goes:
time: 541 us; the launch traced here: 540 us
  waiting for transfers between devices  323 us (60%)
  blocking collectives  100 us (18%)
  local copies, waits for them, and re-layouts  41.1 us (8%)
  matrix products  40.5 us (7%)
  other arithmetic  16 us (3%)
  between operations  13.5 us (2%)
  starting transfers between devices  5.87 us (1%)
    reduce_scatter x1, waiting for transfers between devices, local(): lax.psum_scatter(partial_value.astype(jnp.bfloat16), 'width', scatter_dim...  125 us
    all_gather x1, waiting for transfers between devices, local(): arrived = lax.all_gather(arrived_cols, 'width', axis=3, tiled=True)  105 us
    all_to_all x1, blocking collectives, local(): lax.all_to_all(own_cols, 'expert', split_axis=0, concat_axis=0, tiled=True)  100 us
    all_to_all x1, waiting for transfers between devices, local(): lax.all_to_all(reduced.astype(jnp.bfloat16), 'expert', split_axis=0, conc...  93 us
    dot_general x1, matrix products, local(): jnp.einsum('skmf,kfd->skmd', hidden, down_weight, preferred_element_type=...  15.2 us
    gather x1, local copies, waits for them, and re-layouts, local(): outgoing = padded[table].reshape(n_expert, exp_local, slots, width_all)  14.3 us
    dot_general x1, matrix products, local(): jnp.einsum('skmd,kdf->skmf', arrived, up_weight, preferred_element_type=j...  14.1 us
    dot_general x1, matrix products, local(): jnp.einsum('skmd,kdf->skmf', arrived, gate_weight, preferred_element_type...  11.2 us
  transfers between devices with their start and end apart: 3, of which 3 were waited for; matrix products, arithmetic and copies ran while one was open for 0% of the time, Pallas kernels for 0%

commit v1 on v0

--- a/solution.py
+++ b/solution.py
@@ -26,7 +26,15 @@
     outgoing = padded[table].reshape(n_expert, exp_local, slots, width_all)
     own_cols = lax.dynamic_slice_in_dim(outgoing, lax.axis_index("width") * cols, cols, 3)
     arrived_cols = lax.all_to_all(own_cols, "expert", split_axis=0, concat_axis=0, tiled=True)
-    arrived = lax.all_gather(arrived_cols, "width", axis=3, tiled=True)
+    ways, here = (lax.axis_size("width"), lax.axis_index("width"))
+    grown, reach = (arrived_cols, 1)
+    while reach < ways:
+        theirs = lax.ppermute(grown, "width", [(d, d ^ reach) for d in range(ways)])
+        mine_first = jnp.concatenate([grown, theirs], axis=3)
+        theirs_first = jnp.concatenate([theirs, grown], axis=3)
+        grown = jnp.where(here & reach == 0, mine_first, theirs_first)
+        reach = 2 * reach
+    arrived = grown
     gate = jnp.einsum("skmd,kdf->skmf", arrived, gate_weight, preferred_element_type=jnp.float32)
     up_part = jnp.einsum("skmd,kdf->skmf", arrived, up_weight, preferred_element_type=jnp.float32)
     hidden = (jax.nn.silu(gate) * up_part).astype(jnp.bfloat16)

time: 541 us -> 650 us (1.20)
  waiting for transfers between devices: 323 us -> 406 us
  other arithmetic: 16 us -> 44.7 us
    ppermute x0 -> x2, waiting for transfers between devices: none -> 189 us  [local(): theirs = lax.ppermute(grown, 'width', [(d, d ^ reach) for d in range(ways)])]
    all_gather x1 -> x0, waiting for transfers between devices: 105 us -> none  [local(): arrived = lax.all_gather(arrived_cols, 'width', axis=3, tiled=True)]
    select_n x0 -> x2, other arithmetic: none -> 28.7 us  [local(): grown = jnp.where(here & reach == 0, mine_first, theirs_first)]
  transfers between devices with their start and end apart: 3 -> 4, of which waited for: 3 -> 4; matrix products, arithmetic and copies ran while one was open for 0% -> 0% of each run, Pallas kernels for 0% -> 0%
where the time goes in v1:
time: 650 us; the launch traced here: 649 us
  waiting for transfers between devices  406 us (62%)
  blocking collectives  100 us (15%)
  other arithmetic  44.7 us (7%)
  matrix products  39.1 us (6%)
  local copies, waits for them, and re-layouts  38.7 us (6%)
  between operations  13.5 us (2%)
  starting transfers between devices  7.03 us (1%)
    ppermute x2, waiting for transfers between devices, local(): theirs = lax.ppermute(grown, 'width', [(d, d ^ reach) for d in range(ways)])  189 us
    reduce_scatter x1, waiting for transfers between devices, local(): lax.psum_scatter(partial_value.astype(jnp.bfloat16), 'width', scatter_dim...  124 us
    all_to_all x1, blocking collectives, local(): lax.all_to_all(own_cols, 'expert', split_axis=0, concat_axis=0, tiled=True)  100 us
    all_to_all x1, waiting for transfers between devices, local(): lax.all_to_all(reduced.astype(jnp.bfloat16), 'expert', split_axis=0, conc...  93 us
    select_n x2, other arithmetic, local(): grown = jnp.where(here & reach == 0, mine_first, theirs_first)  28.7 us
    dot_general x1, matrix products, local(): jnp.einsum('skmf,kfd->skmd', hidden, down_weight, preferred_element_type=...  14.6 us
    gather x1, local copies, waits for them, and re-layouts, local(): outgoing = padded[table].reshape(n_expert, exp_local, slots, width_all)  14.3 us
  transfers between devices with their start and end apart: 4, of which 4 were waited for; matrix products, arithmetic and copies ran while one was open for 0% of the time, Pallas kernels for 0%

profile of v1, /device:TPU:0, one launch (start us, length us, event | category | flops | bytes accessed | tf_op | source)
XLA Modules:
  0.0 649.3 jit_solution(18395031242053062087)
XLA Ops:
  6.5 0.8 copy.21
  7.3 0.1 eq.37
  7.4 0.1 eq.33
  7.5 0.7 broadcast_multiply_fusion
  8.2 4.5 reduce-window.6
  12.7 0.1 slice.12
  12.8 0.1 copy.23
  13.0 0.1 copy.24
  13.1 0.1 broadcast_add_fusion
  13.2 0.1 copy.20
  13.3 0.1 mul.40
  13.4 4.3 scatter_custom_fusion
  17.7 1.3 concatenate.15
  19.1 14.3 %gather_fusion = bf16[2048,4096]{1,0:T(8,128)(2,1)} fusion(bf16[129,4096]{1,0:T(8,128)(2,1)S(1)} %concatenate.15, s32[2048]{0:T(1024)S(1)} %fusion.19), kind=kCustom, calls=%fused_computation | custom fusion | bytes 33562624 | tf_op jit(solution)/shard_map/gather | solution.py:26
  33.4 2.6 constant_dynamic-slice_fusion
  36.0 100.4 %all_to_all.10 = bf16[8,2,128,1024]{3,2,1,0:T(8,128)(2,1)} all-to-all(bf16[8,2,128,1024]{3,2,1,0:T(8,128)(2,1)S(1)} %constant_dynamic-slice_fusion), channel_id=1, replica_groups=mesh['expert'=8,'width'=4] {'expert'}, dimensions={0} | all-to-all | bytes 8388608 | tf_op jit(solution)/shard_map/all_to_all | solution.py:28
  136.4 7.5 %collective-permute-done = bf16[8,2,128,1024]{3,2,1,0:T(8,128)(2,1)} collective-permute-done((bf16[8,2,128,1024]{3,2,1,0:T(8,128)(2,1)}, bf16[8,2,128,1024]{3,2,1,0:T(8,128)(2,1)}, u32[]{:S(2)}, u32[]{:S(2)}) %collective-permute-start) | collective-permute-done | bytes 4194336 | tf_op jit(solution)/shard_map/ppermute | solution.py:32
  143.9 11.2 %maximum_select_fusion.1 = bf16[8,2,128,2048]{3,2,1,0:T(8,128)(2,1)} fusion(bf16[8,2,128,1024]{3,2,1,0:T(8,128)(2,1)} %collective-permute-done, bf16[8,2,128,1024]{3,2,1,0:T(8,128)(2,1)} %all_to_all.10, pred[]{:T(512)S(6)} %eq.32), kind=kLoop, calls=%fused_computation.9 | loop fusion | flops 37748736 | bytes 16777216 | tf_op jit(solution)/shard_map/jit(_where)/select_n | solution.py:35
  155.1 1.5 collective-permute-start.1
  156.7 181.3 %collective-permute-done.1 = bf16[8,2,128,2048]{3,2,1,0:T(8,128)(2,1)} collective-permute-done((bf16[8,2,128,2048]{3,2,1,0:T(8,128)(2,1)}, bf16[8,2,128,2048]{3,2,1,0:T(8,128)(2,1)}, u32[]{:S(2)}, u32[]{:S(2)}) %collective-permute-start.1) | collective-permute-done | bytes 8388640 | tf_op jit(solution)/shard_map/ppermute | solution.py:32
  337.9 17.4 %maximum_select_fusion = bf16[8,2,128,4096]{3,2,1,0:T(8,128)(2,1)S(1)} fusion(bf16[8,2,128,2048]{3,2,1,0:T(8,128)(2,1)} %collective-permute-done.1, bf16[8,2,128,2048]{3,2,1,0:T(8,128)(2,1)} %maximum_select_fusion.1, pred[]{:T(512)S(6)} %eq.31), kind=kLoop, calls=%fused_computation.3 | loop fusion | flops 75497472 | bytes 33554432 | tf_op jit(solution)/shard_map/jit(_where)/select_n | solution.py:35
  355.4 12.0 %fusion.2 = f32[2,8,128,384]{3,2,1,0:T(8,128)} fusion(bf16[8,2,128,4096]{3,2,1,0:T(8,128)(2,1)S(1)} %maximum_select_fusion, bf16[2,4096,384]{2,1,0:T(8,128)(2,1)} %param.9), kind=kOutput, calls=%fused_computation.7 | convolution fusion | flops 6442450944 | bytes 26214400 | tf_op jit(solution)/shard_map/skmd,kdf->skmf/dot_general | solution.py:38
  367.4 12.5 %fusion.8 = bf16[8,2,128,384]{3,2,0,1:T(8,128)(2,1)} fusion(f32[2,8,128,384]{3,2,1,0:T(8,128)} %fusion.2, bf16[2,4096,384]{2,1,0:T(8,128)(2,1)} %param.10, bf16[8,2,128,4096]{3,2,1,0:T(8,128)(2,1)S(1)} %maximum_select_fusion), kind=kOutput, calls=%fused_computation.17 | convolution fusion | flops 6447169536 | bytes 27787264 | tf_op jit(solution)/shard_map/skmd,kdf->skmf/dot_general | solution.py:39
  379.9 14.6 %convert_bitcast_fusion = bf16[8,2,128,4096]{3,2,0,1:T(8,128)(2,1)} fusion(bf16[8,2,128,384]{3,2,0,1:T(8,128)(2,1)} %fusion.8, bf16[2,384,4096]{2,1,0:T(8,128)(2,1)} %param.11), kind=kOutput, calls=%fused_computation.4 | convolution fusion | flops 6450839552 | bytes 24641536 | tf_op jit(solution)/shard_map/skmf,kfd->skmd/dot_general | solution.py:41
  394.5 124.1 %reduce-scatter.2.cloned.1.call-done = bf16[8,2,128,1024]{3,2,0,1:T(8,128)(2,1)} async-done(((bf16[8,2,128,4096]{3,2,0,1:T(8,128)(2,1)}), bf16[8,2,128,1024]{3,2,0,1:T(8,128)(2,1)}) %reduce-scatter.2.cloned.1.call-update) | async-done | bytes 4194320 | tf_op jit(solution)/shard_map/reduce_scatter | solution.py:44
  518.6 4.7 copy.27
  523.4 5.5 all-to-all-start.1
  528.9 0.1 copy.19
  529.0 93.0 %all-to-all-done.1 = bf16[8,2,128,1024]{3,2,1,0:T(8,128)(2,1)} async-done(((bf16[8,2,128,1024]{3,2,1,0:T(8,128)(2,1)}), bf16[8,2,128,1024]{3,2,1,0:T(8,128)(2,1)}, u32[]{:S(2)}, u32[]{:S(2)}) %all-to-all-start.1) | async-done | bytes 4194336 | tf_op jit(solution)/shard_map/all_to_all | solution.py:47
  622.0 6.5 bitcast_convert_fusion
  628.5 9.8 %gather_fusion.1 = f32[1024,1024]{1,0:T(8,128)} fusion(f32[2048,1024]{1,0:T(8,128)} %bitcast_convert_fusion, s32[1024]{0:T(1024)S(1)} %broadcast_clamp_fusion), kind=kCustom, calls=%fused_computation.1 | custom fusion | bytes 8392704 | tf_op jit(solution)/shard_map/gather | solution.py:50
  638.3 4.2 fusion.7
  (14 shorter events, 0.1 us)
Async XLA Ops:
  6.5 512.1 %reduce-scatter.2.cloned.1.call-start = ((), (), s32[]{:S(2)}) async-start(), calls=%async_computation.3 | async-start | bytes 20971520 | tf_op jit(solution)/shard_map/reduce_scatter | solution.py:44
  136.4 7.5 %collective-permute-start = (bf16[8,2,128,1024]{3,2,1,0:T(8,128)(2,1)}, bf16[8,2,128,1024]{3,2,1,0:T(8,128)(2,1)}, u32[]{:S(2)}, u32[]{:S(2)}) collective-permute-start(bf16[8,2,128,1024]{3,2,1,0:T(8,128)(2,1)} %all_to_all.10), channel_id=1, source_target_pairs={{0,1},{1,0},{2,3},{3,2},{4,5},{5,4},{6,7},{7,6},{8,9},{9,8},{10,11... | collective-permute-start | bytes 12582920 | tf_op jit(solution)/shard_map/ppermute | solution.py:32
  155.1 182.8 %collective-permute-start.1 = (bf16[8,2,128,2048]{3,2,1,0:T(8,128)(2,1)}, bf16[8,2,128,2048]{3,2,1,0:T(8,128)(2,1)}, u32[]{:S(2)}, u32[]{:S(2)}) collective-permute-start(bf16[8,2,128,2048]{3,2,1,0:T(8,128)(2,1)} %maximum_select_fusion.1), channel_id=1, source_target_pairs={{0,2},{1,3},{2,0},{3,1},{4,6},{5,7},{6,4},{7,5},{8,10},{9,11},{10,... | collective-permute-start | bytes 25165832 | tf_op jit(solution)/shard_map/ppermute | solution.py:32
  394.5 134.4 %copy-start = (f32[128,8]{0,1:T(8,128)S(1)}, f32[128,8]{0,1:T(8,128)}, u32[]{:S(2)}) copy-start(f32[128,8]{0,1:T(8,128)} %param.8) | copy-start | bytes 12292
  523.4 98.6 %all-to-all-start.1 = ((bf16[8,2,128,1024]{3,2,1,0:T(8,128)(2,1)}), bf16[8,2,128,1024]{3,2,1,0:T(8,128)(2,1)}, u32[]{:S(2)}, u32[]{:S(2)}) async-start(bf16[8,2,128,1024]{3,2,1,0:T(8,128)(2,1)} %copy.27), calls=%async_computation.2 | async-start | bytes 8388608 | tf_op jit(solution)/shard_map/all_to_all | solution.py:47
Sparse Core Ops, SparseCore 0:
  394.6 123.9 reduce-scatter.1
